TPU v7x, 32 devices: a whole 2x2x4 slice. The times are simulated.
32 devices in a mesh: col: 16 (over z, x, core), tok: 2 (over y).
Axes of the slice: x: 2, y: 2, z: 4, core: 2. Of those that a mesh axis runs over, the one named last changes fastest.
Arguments:
- acts: bfloat16 [512, 8192], P('tok', 'col'), may hold values from -6 to 6
- grad_out: bfloat16 [512, 8192], P('tok', 'col'), may hold values from -0.19921875 to 0.19921875
- left_factor: float32 [8, 8192, 1024], P('tok', 'col'), may hold values from -6 to 6
- right_factor: float32 [8, 8192, 1024], P('tok', 'col'), may hold values from -6 to 6
- left_basis: bfloat16 [8, 8192, 1024], P('tok', 'col'), may hold values from -0.1875 to 0.1875
- right_basis: bfloat16 [8, 8192, 1024], P('tok', 'col'), may hold values from -0.1875 to 0.1875
- moment: float32 [8192, 8192], P('tok', 'col'), may hold values from -2 to 2
- second: float32 [8192, 8192], P('tok', 'col'), may hold values from 0.05 to 2
Outputs:
- left_out: float32 [8, 8192, 1024], P('tok', 'col')
- right_out: float32 [8, 8192, 1024], P('tok', 'col')
- moment_out: float32 [8192, 8192], P('tok', 'col')
- second_out: float32 [8192, 8192], P('tok', 'col')
- update: bfloat16 [8192, 8192], P('tok', 'col')
All inputs are finite; a program needn't handle non-finite values.
Results may differ from a plain program's by a relative error of at most 0.0075.
Values may be sent and summed in bfloat16 or wider, within the bound.
No kernel may reach another device: no remote copies, remote signals or barrier semaphores. Data moves between devices by JAX's collectives and lax.ppermute only.
A program may use at most 192 MiB of HBM per device.

v0:
```python
import functools

import jax
import jax.numpy as jnp
from jax import lax
from jax.experimental import pallas as pl
from jax.experimental.pallas import tpu as pltpu
from jax.sharding import PartitionSpec as P

B = 1024


shampoo_beta = 0.95
first_beta = 0.9
second_beta = 0.95
first_corr = 1.0 - 0.9**4
second_corr = 1.0 - 0.95**4
epsilon = 1e-08

f32 = jnp.float32
bf16 = jnp.bfloat16


def dot(a, b, ca, cb):
    return lax.dot_general(a, b, (((ca,), (cb,)), ((), ())), preferred_element_type=f32)


def swapped(array, axis, distance):
    return lax.ppermute(array, axis, [(i, i ^ 1 << distance) for i in range(lax.axis_size(axis))])


def join_pair(current, incoming, axis, lower):
    width = current.shape[axis]
    shape = list(current.shape)
    shape[axis] = 2 * width
    joined = jnp.zeros(shape, current.dtype)
    mine_at = jnp.where(lower, 0, width)
    theirs_at = width - mine_at
    joined = lax.dynamic_update_slice_in_dim(joined, current, mine_at, axis)
    return lax.dynamic_update_slice_in_dim(joined, incoming, theirs_at, axis)


def normalized(first_new, second_new):
    return (first_new / first_corr / (jnp.sqrt(second_new / second_corr) + epsilon)).astype(bf16)


def general(acts, grad_out, left_factor, right_factor, left_basis, right_basis, moment, second):
    width = grad_out.shape[1]
    blocks = left_factor.shape[0]
    groups = B // width
    nbits = groups.bit_length() - 1
    member = lax.axis_index("col") % groups
    contract = (((0,), (0,)), ((), ()))
    whole = lax.all_gather(acts, "col", axis=1, tiled=True)
    block_rows = lax.all_to_all(whole, "tok", split_axis=1, concat_axis=0, tiled=True)
    all_grads = lax.all_gather(grad_out, "tok", axis=0, tiled=True)
    grad = lax.dot_general(block_rows, all_grads, contract, preferred_element_type=f32)
    own = grad.astype(bf16).reshape(blocks, B, width)
    tiles, left_full, right_full = (own, left_basis, right_basis)
    for bit in range(nbits):
        other = swapped((tiles, left_full, right_full), "col", bit)
        lower = member >> bit & 1 == 0
        tiles = join_pair(tiles, other[0], 2, lower)
        left_full = join_pair(left_full, other[1], 1, lower)
        right_full = join_pair(right_full, other[2], 1, lower)
    right_cols = lax.dynamic_slice_in_dim(right_full, member * width, width, 2)
    mixed = jnp.einsum("nab,nbc->nac", tiles, right_cols, preferred_element_type=f32).astype(bf16)
    lead = lax.dynamic_slice_in_dim(tiles, member * width, width, 1)
    left_new = shampoo_beta * left_factor + (1.0 - shampoo_beta) * jnp.einsum(
        "nab,ncb->nac", lead, tiles, preferred_element_type=f32
    )
    right_new = shampoo_beta * right_factor + (1.0 - shampoo_beta) * jnp.einsum(
        "nat,nab->ntb", own, tiles, preferred_element_type=f32
    )
    rotated = jnp.einsum("nab,nac->nbc", left_full, mixed, preferred_element_type=f32)
    first_new = first_beta * moment.reshape(blocks, B, width) + (1.0 - first_beta) * rotated
    second_new = (
        second_beta * second.reshape(blocks, B, width) + (1.0 - second_beta) * rotated * rotated
    )
    steps_full = normalized(first_new, second_new)
    for bit in range(nbits):
        other_steps = swapped(steps_full, "col", bit)
        lower = member >> bit & 1 == 0
        steps_full = join_pair(steps_full, other_steps, 2, lower)
    back = jnp.einsum("nab,ncb->nac", steps_full, right_basis, preferred_element_type=f32).astype(bf16)
    update = jnp.einsum("nab,nbc->nac", left_full, back, preferred_element_type=f32).astype(bf16)
    rows = blocks * B
    return (
        left_new,
        right_new,
        first_new.reshape(rows, width),
        second_new.reshape(rows, width),
        update.reshape(rows, width),
    )


def early_kernel(half_ref, g0_ref, g1_ref, h0_ref, h1_ref, right_own_ref, right_other_ref, x_ref, full_ref, gram_ref):
    tokens, width = g0_ref.shape
    at = pl.ds(pl.multiple_of(half_ref[0] * width, width), width)
    away = pl.ds(pl.multiple_of((1 - half_ref[0]) * width, width), width)

    @pl.when(pl.program_id(0) == 0)
    def _():
        full_ref[:tokens, at] = g0_ref[...]
        full_ref[tokens:, at] = g1_ref[...]
        full_ref[:tokens, away] = h0_ref[...]
        full_ref[tokens:, away] = h1_ref[...]
        gram_ref[...] = dot(full_ref[...], full_ref[...], 1, 1).astype(bf16)

    x = dot(full_ref[:, at], right_own_ref[0], 1, 0) + dot(full_ref[:, away], right_other_ref[0], 1, 0)
    x_ref[0] = x.astype(bf16)


def early(half, grads, right_own, right_other):
    blocks, width, order = right_own.shape
    tokens = 2 * grads[0].shape[0]
    whole = lambda n, s: (0, 0)
    column = pl.BlockSpec((1, width, width), lambda n, s: (n, 0, s[0]))
    return pl.pallas_call(
        early_kernel,
        grid_spec=pltpu.PrefetchScalarGridSpec(
            num_scalar_prefetch=1,
            grid=(blocks,),
            in_specs=[pl.BlockSpec((tokens // 2, width), whole)] * 4 + [column, column],
            out_specs=[
                pl.BlockSpec((1, tokens, width), lambda n, s: (n, 0, 0)),
                pl.BlockSpec((tokens, order), whole),
                pl.BlockSpec((tokens, tokens), whole),
            ],
        ),
        out_shape=[
            jax.ShapeDtypeStruct((blocks, tokens, width), bf16),
            jax.ShapeDtypeStruct((tokens, order), bf16),
            jax.ShapeDtypeStruct((tokens, tokens), bf16),
        ],
        compiler_params=pltpu.CompilerParams(vmem_limit_bytes=60 << 20),
        cost_estimate=pl.CostEstimate(
            flops=2 * blocks * tokens * order * width + 2 * tokens * tokens * order,
            bytes_accessed=2 * blocks * width * (order + tokens) + 4 * tokens * order,
            transcendentals=0,
        ),
        name="early",
    )(half, *grads, right_own, right_other)


def step_kernel(count, scal_ref, *refs):
    quads = refs[: 4 * count]
    (full_ref, gram_ref, x_ref, ql_own_ref, ql_other_ref, lf_ref, rf_ref, mo_ref, se_ref) = refs[
        4 * count : 4 * count + 9
    ]
    lo_ref, ro_ref, mout_ref, sout_ref, norm_ref, acts, left, right, mixed = refs[-9:]
    n, s = pl.program_id(0), pl.program_id(1)
    tokens, width = quads[0].shape
    half = scal_ref[0]
    at = pl.ds(pl.multiple_of(half * width, width), width)
    away = pl.ds(pl.multiple_of((1 - half) * width, width), width)

    for m in range(count):

        @pl.when((s == 0) & (n == m))
        def _():
            acts[:tokens, at] = quads[4 * m][...]
            acts[tokens:, at] = quads[4 * m + 1][...]
            acts[:tokens, away] = quads[4 * m + 2][...]
            acts[tokens:, away] = quads[4 * m + 3][...]

    @pl.when(s == 0)
    def _():
        a = acts[...]
        mixed[...] = dot(a, x_ref[0], 0, 0).astype(bf16)
        gram = dot(a, a, 1, 1).astype(bf16)
        left[...] = dot(acts[:, at], gram_ref[...], 0, 0).astype(bf16)
        right[...] = dot(full_ref[:, at], gram, 0, 0).astype(bf16)

    piece = mout_ref.shape[1]
    part = pl.ds(pl.multiple_of(s * piece, piece), piece)
    rot = dot(ql_own_ref[0], mixed[at, :], 0, 0) + dot(ql_other_ref[0], mixed[away, :], 0, 0)
    first_new = first_beta * mo_ref[0] + (1.0 - first_beta) * rot
    second_new = second_beta * se_ref[0] + (1.0 - second_beta) * rot * rot
    mout_ref[0] = first_new
    sout_ref[0] = second_new
    norm_ref[0] = normalized(first_new, second_new)
    lo_ref[0] = shampoo_beta * lf_ref[0] + (1.0 - shampoo_beta) * dot(left[...], acts[:, part], 1, 0)
    ro_ref[0] = shampoo_beta * rf_ref[0] + (1.0 - shampoo_beta) * dot(right[...], full_ref[:, part], 1, 0)


def step_blocks(scal, quads, shared, per_block, carried, pieces=2):
    count = len(quads)
    full, gram, x = shared
    lf, rf, mo, se = per_block[2:]
    tokens, order = full.shape
    _, width, _ = lf.shape
    piece = order // pieces
    factor = pl.BlockSpec((1, width, piece), lambda n, s, c: (c[1 + n], 0, s))
    moment = pl.BlockSpec((1, piece, width), lambda n, s, c: (c[1 + n], s, 0))
    once = lambda shape: pl.BlockSpec(shape, lambda n, s, c: (0, 0), pipeline_mode=pl.Buffered(1))
    in_specs = [once((tokens // 2, width))] * (4 * count) + [once((tokens, order)), once((tokens, tokens))]
    in_specs += [pl.BlockSpec((1, tokens, width), lambda n, s, c: (c[1 + n], 0, 0))]
    in_specs += [factor, factor, factor, factor, moment, moment]
    in_specs += [pl.BlockSpec(memory_space=pl.ANY)] * len(carried)
    first_carried = 1 + 4 * count + 9

    def kernel(*refs):
        at = first_carried
        step_kernel(count, *refs[:at], *refs[at + len(carried) :])

    shapes = [(lf.shape, f32), (rf.shape, f32), (mo.shape, f32), (se.shape, f32), ((count, order, width), bf16)]
    unit = 2 * tokens * tokens * width
    return pl.pallas_call(
        kernel,
        grid_spec=pltpu.PrefetchScalarGridSpec(
            num_scalar_prefetch=1,
            grid=(count, pieces),
            in_specs=in_specs,
            out_specs=[factor, factor, moment, moment, pl.BlockSpec((1, piece, width), lambda n, s, c: (n, s, 0))],
            scratch_shapes=[
                pltpu.VMEM((tokens, order), bf16),
                pltpu.VMEM((width, tokens), bf16),
                pltpu.VMEM((width, tokens), bf16),
                pltpu.VMEM((order, width), bf16),
            ],
        ),
        out_shape=[jax.ShapeDtypeStruct(*a) for a in shapes],
        input_output_aliases={first_carried + i: i for i in range(len(carried))},
        compiler_params=pltpu.CompilerParams(vmem_limit_bytes=60 << 20),
        cost_estimate=pl.CostEstimate(
            flops=14 * count * unit,
            bytes_accessed=count * 18 * order * width,
            transcendentals=2 * count * order * width,
        ),
        name="step",
    )(scal, *[a for q in quads for a in q], full, gram, x, *per_block, *carried)


def update_kernel(carried, scal_ref, n_own_ref, n_other_ref, q_own_ref, q_other_ref, ql_own_ref, ql_other_ref, *rest):
    out_ref, back = rest[carried:]
    width = q_own_ref.shape[1]
    half = scal_ref[0]
    b = dot(n_own_ref[0], q_own_ref[0], 1, 1) + dot(n_other_ref[0], q_other_ref[0], 1, 1)
    back[...] = b.astype(bf16)
    at = pl.ds(pl.multiple_of(half * width, width), width)
    away = pl.ds(pl.multiple_of((1 - half) * width, width), width)
    out_ref[0, at, :] = dot(ql_own_ref[0], back[...], 1, 0).astype(bf16)
    out_ref[0, away, :] = dot(ql_other_ref[0], back[...], 1, 0).astype(bf16)


def update_blocks(scal, norm_own, norm_other, right_own, ql_own, ql_other, carried):
    count, order, width = norm_own.shape
    blocks = ql_own.shape[0]
    stepped = pl.BlockSpec((1, order, width), lambda n, c: (n, 0, 0))
    basis = pl.BlockSpec((1, width, order), lambda n, c: (c[1 + n], 0, 0))
    unit = 2 * width * width * width
    return pl.pallas_call(
        functools.partial(update_kernel, len(carried)),
        grid_spec=pltpu.PrefetchScalarGridSpec(
            num_scalar_prefetch=1,
            grid=(count,),
            in_specs=[
                stepped,
                stepped,
                pl.BlockSpec((1, width, width), lambda n, c: (c[1 + n], 0, c[0])),
                pl.BlockSpec((1, width, width), lambda n, c: (c[1 + n], 0, 1 - c[0])),
                basis,
                basis,
            ]
            + [pl.BlockSpec(memory_space=pl.ANY)] * len(carried),
            out_specs=pl.BlockSpec((1, order, width), lambda n, c: (c[1 + n], 0, 0)),
            scratch_shapes=[pltpu.VMEM((order, width), bf16)],
        ),
        out_shape=jax.ShapeDtypeStruct((blocks, order, width), bf16),
        input_output_aliases={7: 0} if carried else {},
        compiler_params=pltpu.CompilerParams(vmem_limit_bytes=56 << 20),
        cost_estimate=pl.CostEstimate(
            flops=8 * count * unit, bytes_accessed=count * 8 * order * width, transcendentals=0
        ),
        name="update",
    )(scal, norm_own, norm_other, right_own, right_own, ql_own, ql_other, *carried)


def cube(acts, grad_out, left_factor, right_factor, left_basis, right_basis, moment, second):
    _, width = grad_out.shape
    blocks = left_factor.shape[0]
    size = lax.axis_size("col")
    col, y = lax.axis_index("col"), lax.axis_index("tok")
    half = col & 1
    high = col >> (size.bit_length() - 2) & 1
    first_block = (col >> 1 & (blocks - 1)) ^ jnp.where(high == y, 0, 2)

    def hop(array, mask):
        return lax.ppermute(array, "col", [(i, i ^ mask) for i in range(size)])

    def across(array):
        return lax.ppermute(array, "tok", [(0, 1), (1, 0)])

    core = lambda array: hop(array, 1)
    x_hop = lambda array: hop(array, 2)
    a_hop = lambda array: hop(array, 4)
    inner = high == y
    mirrored = hop(acts, size - 4)
    grads_away = across(grad_out)
    q_other = core(right_basis)
    ql_other = core(left_basis)
    grads = (grad_out, grads_away, core(grad_out), core(grads_away))
    near = jnp.where(inner, acts, mirrored)
    far = across(jnp.where(inner, mirrored, acts))
    near_x, near_a = x_hop(near), a_hop(near)
    far_x, far_a = x_hop(far), a_hop(far)
    near_d, far_d = x_hop(near_a), hop(far, 6)
    quad = lambda n, f: (n, f, core(n), core(f))
    quad0, quad_x, quad_a, quad_d = quad(near, far), quad(near_x, far_x), quad(near_a, far_a), quad(near_d, far_d)

    as_scal = lambda *v: jnp.stack([jnp.asarray(a, jnp.int32) for a in v])
    s0 = as_scal(half, first_block)
    s1 = as_scal(half, first_block ^ 1, first_block ^ 2, first_block ^ 3)
    x, full, gram = early(s0, grads, right_basis, q_other)
    shared = (full, gram, x)
    shaped = (blocks, B, width)
    states = (left_factor, right_factor, moment.reshape(shaped), second.reshape(shaped))
    per_block = (left_basis, ql_other, *states)
    *outs, norm0 = step_blocks(s0, [quad0], shared, per_block, [])
    *outs, norm1 = step_blocks(s1, [quad_x, quad_a, quad_d], shared, per_block, outs)
    away0, away1 = core(norm0), core(norm1)
    update = update_blocks(s0, norm0, away0, right_basis, left_basis, ql_other, [])
    update = update_blocks(s1, norm1, away1, right_basis, left_basis, ql_other, [update])
    rows = blocks * B
    left_new, right_new, first_new, second_new = outs
    return (
        left_new,
        right_new,
        first_new.reshape(rows, width),
        second_new.reshape(rows, width),
        update.reshape(rows, width),
    )


def shards(acts, grad_out, *rest):
    blocks = rest[0].shape[0]
    pairs = B // grad_out.shape[1] == 2 and lax.axis_size("tok") == 2
    if pairs and blocks == 4 and lax.axis_size("col") == 4 * blocks:
        return cube(acts, grad_out, *rest)
    return general(acts, grad_out, *rest)


def solution(mesh):
    in_specs = (
        P("tok", "col"),
        P("tok", "col"),
        P("tok", "col", None),
        P("tok", "col", None),
        P("tok", "col", None),
        P("tok", "col", None),
        P("tok", "col"),
        P("tok", "col"),
    )
    out_specs = (
        P("tok", "col", None),
        P("tok", "col", None),
        P("tok", "col"),
        P("tok", "col"),
        P("tok", "col"),
    )
    return jax.shard_map(shards, mesh=mesh, in_specs=in_specs, out_specs=out_specs, check_vma=False)
```

profile of v0, /device:TPU:0, one launch (start us, length us, event | category | flops | bytes accessed | tf_op | source)
XLA Modules:
  0.0 126.5 jit_solution(5274375528665718483)
XLA Ops:
  0.6 0.6 collective-permute-start.17
  1.2 0.1 collective-permute-start.18
  1.3 5.0 %collective-permute-start = (bf16[256,512]{1,0:T(8,128)(2,1)}, bf16[256,512]{1,0:T(8,128)(2,1)S(1)}, u32[]{:S(2)}, u32[]{:S(2)}) collective-permute-start(bf16[256,512]{1,0:T(8,128)(2,1)} %param.8), channel_id=1, source_target_pairs={{0,24},{2,26},{4,28},{6,30},{8,16},{10,18},{12,20},{14,22},{16,8},... | collective-permute-start | bytes 786440 | tf_op jit(solution)/shard_map/ppermute | solution.py:290
  6.3 1.5 %collective-permute-start.14 = (bf16[256,512]{1,0:T(8,128)(2,1)}, bf16[256,512]{1,0:T(8,128)(2,1)S(1)}, u32[]{:S(2)}, u32[]{:S(2)}) collective-permute-start(bf16[256,512]{1,0:T(8,128)(2,1)} %g0_ref.1), channel_id=1, source_target_pairs={{0,1},{1,0},{2,3},{3,2},{4,5},{5,4},{6,7},{7,6},{8,9},{9,8},{10,11... | collective-permute-start | bytes 786440 | tf_op jit(solution)/shard_map/ppermute | solution.py:293
  7.8 5.3 %collective-permute-done = bf16[256,512]{1,0:T(8,128)(2,1)S(1)} collective-permute-done((bf16[256,512]{1,0:T(8,128)(2,1)}, bf16[256,512]{1,0:T(8,128)(2,1)S(1)}, u32[]{:S(2)}, u32[]{:S(2)}) %collective-permute-start) | collective-permute-done | bytes 262176 | tf_op jit(solution)/shard_map/ppermute | solution.py:290
  13.1 1.0 broadcast_select_fusion
  14.1 1.6 %collective-permute-start.2 = (bf16[256,512]{1,0:T(8,128)(2,1)S(1)}, bf16[256,512]{1,0:T(8,128)(2,1)S(1)}, u32[]{:S(2)}, u32[]{:S(2)}) collective-permute-start(bf16[256,512]{1,0:T(8,128)(2,1)S(1)} %get-tuple-element.31), channel_id=1, source_target_pairs={{0,1},{1,0},{2,3},{3,2},{4,5},{5,4},{6,7},{7,6},{8,9},{9,8},{10,11... | collective-permute-start | bytes 786440 | tf_op jit(solution)/shard_map/ppermute | solution.py:293
  15.7 0.0 collective-permute-done.15.h0_ref
  15.8 0.0 copy-start.18
  15.8 5.3 %collective-permute-start.6 = (bf16[256,512]{1,0:T(8,128)(2,1)S(1)}, bf16[256,512]{1,0:T(8,128)(2,1)S(1)}, u32[]{:S(2)}, u32[]{:S(2)}) collective-permute-start(bf16[256,512]{1,0:T(8,128)(2,1)S(1)} %get-tuple-element.32.refs_1_), channel_id=1, source_target_pairs={{0,8},{2,10},{4,12},{6,14},{8,0},{10,2},{12,4},{14,6},{16,24},{18,... | collective-permute-start | bytes 786440 | tf_op jit(solution)/shard_map/ppermute | solution.py:290
  21.1 0.8 collective-permute-done.2.refs_2_
  21.9 1.3 %collective-permute-start.1 = (bf16[256,512]{1,0:T(8,128)(2,1)S(1)}, bf16[256,512]{1,0:T(8,128)(2,1)S(1)}, u32[]{:S(2)}, u32[]{:S(2)}) collective-permute-start(bf16[256,512]{1,0:T(8,128)(2,1)S(1)} %get-tuple-element.32.refs_1_), channel_id=1, source_target_pairs={{0,4},{2,6},{4,0},{6,2},{8,12},{10,14},{12,8},{14,10},{16,20},{18,... | collective-permute-start | bytes 786440 | tf_op jit(solution)/shard_map/ppermute | solution.py:290
  23.2 0.0 collective-permute-start.16
  23.2 4.8 %collective-permute-done.6.refs_5_ = bf16[256,512]{1,0:T(8,128)(2,1)S(1)} collective-permute-done((bf16[256,512]{1,0:T(8,128)(2,1)S(1)}, bf16[256,512]{1,0:T(8,128)(2,1)S(1)}, u32[]{:S(2)}, u32[]{:S(2)}) %collective-permute-start.6) | collective-permute-done | bytes 262176 | tf_op jit(solution)/shard_map/ppermute | solution.py:290
  28.0 0.0 collective-permute-start.20
  28.0 1.5 %collective-permute-done.1.refs_1_ = bf16[256,512]{1,0:T(8,128)(2,1)S(1)} collective-permute-done((bf16[256,512]{1,0:T(8,128)(2,1)S(1)}, bf16[256,512]{1,0:T(8,128)(2,1)S(1)}, u32[]{:S(2)}, u32[]{:S(2)}) %collective-permute-start.1) | collective-permute-done | bytes 262176 | tf_op jit(solution)/shard_map/ppermute | solution.py:290
  29.4 5.0 %collective-permute-start.11 = (bf16[256,512]{1,0:T(8,128)(2,1)S(1)}, bf16[256,512]{1,0:T(8,128)(2,1)S(1)}, u32[]{:S(2)}, u32[]{:S(2)}) collective-permute-start(bf16[256,512]{1,0:T(8,128)(2,1)S(1)} %collective-permute-done.2.refs_2_), channel_id=1, source_target_pairs={{0,12},{2,14},{4,8},{6,10},{8,4},{10,6},{12,0},{14,2},{16,28},{18,... | collective-permute-start | bytes 786440 | tf_op jit(solution)/shard_map/ppermute | solution.py:290
  34.4 0.6 pad_add_fusion.1.half_ref.refs_0_.scal_ref
  35.0 0.6 collective-permute-start.3
  35.6 5.6 %collective-permute-done.11.refs_10_ = bf16[256,512]{1,0:T(8,128)(2,1)S(1)} collective-permute-done((bf16[256,512]{1,0:T(8,128)(2,1)S(1)}, bf16[256,512]{1,0:T(8,128)(2,1)S(1)}, u32[]{:S(2)}, u32[]{:S(2)}) %collective-permute-start.11) | collective-permute-done | bytes 262176 | tf_op jit(solution)/shard_map/ppermute | solution.py:290
  41.2 0.7 collective-permute-start.10
  42.0 0.0 collective-permute-done.17.right_other_ref
  42.0 0.0 collective-permute-start.8
  42.0 0.7 pad_add_fusion.refs_0_.scal_ref
  42.6 7.5 %early.1 = (bf16[4,512,512]{2,1,0:T(8,128)(2,1)}, bf16[512,1024]{1,0:T(8,128)(2,1)}, bf16[512,512]{1,0:T(8,128)(2,1)}) custom-call(s32[2]{0:T(128)} %pad_add_fusion.1.half_ref.refs_0_.scal_ref, bf16[256,512]{1,0:T(8,128)(2,1)} %g0_ref.1, bf16[256,512]{1,0:T(8,128)(2,1)} %copy-done.17, bf16[256,512]{1,0:T(8,128)(2,1)} %copy-done.18, ...), custom_call_target="tpu_custom_call" | custom-call | flops 2684354560 | bytes 8388608 | tf_op jit(solution)/shard_map/early/pallas_call | solution.py:119
  50.1 0.6 collective-permute-start.4
  50.7 0.1 collective-permute-start.13
  50.8 0.0 collective-permute-done.10.refs_9_
  50.8 0.4 collective-permute-start.9
  51.2 0.0 collective-permute-done.8.refs_7_
  51.3 0.1 collective-permute-start.5
  51.3 0.0 collective-permute-done.18.refs_9_.refs_17_.ql_other_ref
  51.3 0.4 collective-permute-start.12
  51.8 12.4 %step.2 = (f32[4,512,1024]{2,1,0:T(8,128)}, f32[4,512,1024]{2,1,0:T(8,128)}, f32[4,1024,512]{2,1,0:T(8,128)}, f32[4,1024,512]{2,1,0:T(8,128)}, bf16[1,1024,512]{2,1,0:T(8,128)(2,1)}) custom-call(s32[2]{0:T(128)} %pad_add_fusion.1.half_ref.refs_0_.scal_ref, bf16[256,512]{1,0:T(8,128)(2,1)} %copy-done.1, bf16[256,512]{1,0:T(8,128)(2,1)} %copy-done.6, ...), custom_call_target="tpu_custom_call" | custom-call | flops 3758096384 | bytes 9437184 | tf_op jit(solution)/shard_map/step/pallas_call | solution.py:209
  64.3 0.0 collective-permute-done.9.refs_8_
  64.3 0.0 collective-permute-done.5.refs_4_
  64.3 0.7 copy-done.15
  65.0 0.1 copy-done.16
  65.1 0.0 copy-done.14
  65.2 32.9 %step.3 = (f32[4,512,1024]{2,1,0:T(8,128)}, f32[4,512,1024]{2,1,0:T(8,128)}, f32[4,1024,512]{2,1,0:T(8,128)}, f32[4,1024,512]{2,1,0:T(8,128)}, bf16[3,1024,512]{2,1,0:T(8,128)(2,1)}) custom-call(s32[4]{0:T(128)} %pad_add_fusion.refs_0_.scal_ref, ...), custom_call_target="tpu_custom_call", output_to_operand_aliasing={{0}: (22, {}), {1}: (23, {}), {2}: (24, {}), {3}: (25, {})} | custom-call | flops 11274289152 | bytes 28311552 | tf_op jit(solution)/shard_map/step/pallas_call | solution.py:209
  98.1 0.2 collective-permute-start.21
  98.3 0.4 collective-permute-start.22
  98.6 6.9 %collective-permute-done.22.n_other_ref = bf16[1,1024,512]{2,1,0:T(8,128)(2,1)S(1)} collective-permute-done((bf16[1,1024,512]{2,1,0:T(8,128)(2,1)S(1)}, bf16[1,1024,512]{2,1,0:T(8,128)(2,1)S(1)}, u32[]{:S(2)}, u32[]{:S(2)}) %collective-permute-start.22) | collective-permute-done | bytes 1048608 | tf_op jit(solution)/shard_map/ppermute | solution.py:290
  105.5 1.0 copy-done.3
  106.5 6.5 %update.2.rest_0_ = bf16[4,1024,512]{2,1,0:T(8,128)(2,1)} custom-call(s32[2]{0:T(128)} %pad_add_fusion.1.half_ref.refs_0_.scal_ref, bf16[1,1024,512]{2,1,0:T(8,128)(2,1)} %get-tuple-element.30.n_own_ref, bf16[1,1024,512]{2,1,0:T(8,128)(2,1)} %copy-done.3, bf16[4,512,1024]{2,1,0:T(8,128)(2,1)} %q_other_ref.3, bf16[4,512,1024]{2,1,0:T(8,128)(2,1)} %q_other_ref.3, ...), custom_call_target="tpu_custom_call" | custom-call | flops 2147483648 | bytes 4194304 | tf_op jit(solution)/shard_map/update/pallas_call | solution.py:253
  113.0 0.0 collective-permute-done.21.n_other_ref
  113.0 1.7 %copy-done = bf16[3,1024,512]{2,1,0:T(8,128)(2,1)} copy-done((bf16[3,1024,512]{2,1,0:T(8,128)(2,1)}, bf16[3,1024,512]{2,1,0:T(8,128)(2,1)S(1)}, u32[]{:S(2)}) %copy-start) | copy-done | bytes 3145752
  114.7 11.8 %update.3 = bf16[4,1024,512]{2,1,0:T(8,128)(2,1)} custom-call(s32[4]{0:T(128)} %pad_add_fusion.refs_0_.scal_ref, bf16[3,1024,512]{2,1,0:T(8,128)(2,1)} %get-tuple-element.29.n_own_ref, bf16[3,1024,512]{2,1,0:T(8,128)(2,1)} %copy-done, bf16[4,512,1024]{2,1,0:T(8,128)(2,1)} %q_other_ref.3, ...), custom_call_target="tpu_custom_call", output_to_operand_aliasing={{}: (7, {})} | custom-call | flops 6442450944 | bytes 12582912 | tf_op jit(solution)/shard_map/update/pallas_call | solution.py:253
  (44 shorter events, 0.1 us)
Async XLA Ops:
  0.6 41.3 %collective-permute-start.17 = (bf16[4,512,1024]{2,1,0:T(8,128)(2,1)}, bf16[4,512,1024]{2,1,0:T(8,128)(2,1)}, u32[]{:S(2)}, u32[]{:S(2)}) collective-permute-start(bf16[4,512,1024]{2,1,0:T(8,128)(2,1)} %q_other_ref.3), channel_id=1, source_target_pairs={{0,2},{2,0},{4,6},{6,4},{8,10},{10,8},{12,14},{14,12},{16,18},{18,... | collective-permute-start | bytes 12582920 | tf_op jit(solution)/shard_map/ppermute | solution.py:290
  1.2 50.2 %collective-permute-start.18 = (bf16[4,512,1024]{2,1,0:T(8,128)(2,1)}, bf16[4,512,1024]{2,1,0:T(8,128)(2,1)}, u32[]{:S(2)}, u32[]{:S(2)}) collective-permute-start(bf16[4,512,1024]{2,1,0:T(8,128)(2,1)} %ql_own_ref.3), channel_id=1, source_target_pairs={{0,2},{2,0},{4,6},{6,4},{8,10},{10,8},{12,14},{14,12},{16,18},{18,... | collective-permute-start | bytes 12582920 | tf_op jit(solution)/shard_map/ppermute | solution.py:290
  1.3 11.9 %collective-permute-start = (bf16[256,512]{1,0:T(8,128)(2,1)}, bf16[256,512]{1,0:T(8,128)(2,1)S(1)}, u32[]{:S(2)}, u32[]{:S(2)}) collective-permute-start(bf16[256,512]{1,0:T(8,128)(2,1)} %param.8), channel_id=1, source_target_pairs={{0,24},{2,26},{4,28},{6,30},{8,16},{10,18},{12,20},{14,22},{16,8},... | collective-permute-start | bytes 786440 | tf_op jit(solution)/shard_map/ppermute | solution.py:290
  6.3 9.5 %collective-permute-start.14 = (bf16[256,512]{1,0:T(8,128)(2,1)}, bf16[256,512]{1,0:T(8,128)(2,1)S(1)}, u32[]{:S(2)}, u32[]{:S(2)}) collective-permute-start(bf16[256,512]{1,0:T(8,128)(2,1)} %g0_ref.1), channel_id=1, source_target_pairs={{0,1},{1,0},{2,3},{3,2},{4,5},{5,4},{6,7},{7,6},{8,9},{9,8},{10,11... | collective-permute-start | bytes 786440 | tf_op jit(solution)/shard_map/ppermute | solution.py:293
  7.8 7.9 %collective-permute-start.15 = (bf16[256,512]{1,0:T(8,128)(2,1)}, bf16[256,512]{1,0:T(8,128)(2,1)S(1)}, u32[]{:S(2)}, u32[]{:S(2)}) collective-permute-start(bf16[256,512]{1,0:T(8,128)(2,1)} %g0_ref.1), channel_id=1, source_target_pairs={{0,2},{2,0},{4,6},{6,4},{8,10},{10,8},{12,14},{14,12},{16,18},{18,... | collective-permute-start | bytes 786440 | tf_op jit(solution)/shard_map/ppermute | solution.py:290
  14.1 37.6 %copy-start.1 = (bf16[256,512]{1,0:T(8,128)(2,1)}, bf16[256,512]{1,0:T(8,128)(2,1)S(1)}, u32[]{:S(2)}) copy-start(bf16[256,512]{1,0:T(8,128)(2,1)S(1)} %get-tuple-element.32.refs_1_) | copy-start | bytes 786436
  14.1 7.7 %collective-permute-start.2 = (bf16[256,512]{1,0:T(8,128)(2,1)S(1)}, bf16[256,512]{1,0:T(8,128)(2,1)S(1)}, u32[]{:S(2)}, u32[]{:S(2)}) collective-permute-start(bf16[256,512]{1,0:T(8,128)(2,1)S(1)} %get-tuple-element.31), channel_id=1, source_target_pairs={{0,1},{1,0},{2,3},{3,2},{4,5},{5,4},{6,7},{7,6},{8,9},{9,8},{10,11... | collective-permute-start | bytes 786440 | tf_op jit(solution)/shard_map/ppermute | solution.py:293
  15.7 26.9 %copy-start.17 = (bf16[256,512]{1,0:T(8,128)(2,1)}, bf16[256,512]{1,0:T(8,128)(2,1)S(1)}, u32[]{:S(2)}) copy-start(bf16[256,512]{1,0:T(8,128)(2,1)S(1)} %collective-permute-done.14.g1_ref) | copy-start | bytes 786436
  15.7 7.4 %collective-permute-start.19 = (bf16[256,512]{1,0:T(8,128)(2,1)S(1)}, bf16[256,512]{1,0:T(8,128)(2,1)S(1)}, u32[]{:S(2)}, u32[]{:S(2)}) collective-permute-start(bf16[256,512]{1,0:T(8,128)(2,1)S(1)} %get-tuple-element.32.refs_1_), channel_id=1, source_target_pairs={{0,2},{2,0},{4,6},{6,4},{8,10},{10,8},{12,14},{14,12},{16,18},{18,... | collective-permute-start | bytes 786440 | tf_op jit(solution)/shard_map/ppermute | solution.py:290
  15.8 12.2 %copy-start.18 = (bf16[256,512]{1,0:T(8,128)(2,1)}, bf16[256,512]{1,0:T(8,128)(2,1)S(1)}, u32[]{:S(2)}) copy-start(bf16[256,512]{1,0:T(8,128)(2,1)S(1)} %collective-permute-done.15.h0_ref) | copy-start | bytes 786436
  15.8 12.2 %collective-permute-start.6 = (bf16[256,512]{1,0:T(8,128)(2,1)S(1)}, bf16[256,512]{1,0:T(8,128)(2,1)S(1)}, u32[]{:S(2)}, u32[]{:S(2)}) collective-permute-start(bf16[256,512]{1,0:T(8,128)(2,1)S(1)} %get-tuple-element.32.refs_1_), channel_id=1, source_target_pairs={{0,8},{2,10},{4,12},{6,14},{8,0},{10,2},{12,4},{14,6},{16,24},{18,... | collective-permute-start | bytes 786440 | tf_op jit(solution)/shard_map/ppermute | solution.py:290
  21.9 29.9 %copy-start.6 = (bf16[256,512]{1,0:T(8,128)(2,1)}, bf16[256,512]{1,0:T(8,128)(2,1)S(1)}, u32[]{:S(2)}) copy-start(bf16[256,512]{1,0:T(8,128)(2,1)S(1)} %collective-permute-done.2.refs_2_) | copy-start | bytes 786436
  21.9 7.5 %collective-permute-start.1 = (bf16[256,512]{1,0:T(8,128)(2,1)S(1)}, bf16[256,512]{1,0:T(8,128)(2,1)S(1)}, u32[]{:S(2)}, u32[]{:S(2)}) collective-permute-start(bf16[256,512]{1,0:T(8,128)(2,1)S(1)} %get-tuple-element.32.refs_1_), channel_id=1, source_target_pairs={{0,4},{2,6},{4,0},{6,2},{8,12},{10,14},{12,8},{14,10},{16,20},{18,... | collective-permute-start | bytes 786440 | tf_op jit(solution)/shard_map/ppermute | solution.py:290
  23.2 28.6 %copy-start.7 = (bf16[256,512]{1,0:T(8,128)(2,1)}, bf16[256,512]{1,0:T(8,128)(2,1)S(1)}, u32[]{:S(2)}) copy-start(bf16[256,512]{1,0:T(8,128)(2,1)S(1)} %collective-permute-done.19.refs_3_) | copy-start | bytes 786436
  23.2 11.8 %collective-permute-start.16 = (bf16[256,512]{1,0:T(8,128)(2,1)S(1)}, bf16[256,512]{1,0:T(8,128)(2,1)}, u32[]{:S(2)}, u32[]{:S(2)}) collective-permute-start(bf16[256,512]{1,0:T(8,128)(2,1)S(1)} %collective-permute-done.14.g1_ref), channel_id=1, source_target_pairs={{0,2},{2,0},{4,6},{6,4},{8,10},{10,8},{12,14},{14,12},{16,18},{18,... | collective-permute-start | bytes 786440 | tf_op jit(solution)/shard_map/ppermute | solution.py:290
  28.0 36.2 %copy-start.4 = (bf16[256,512]{1,0:T(8,128)(2,1)}, bf16[256,512]{1,0:T(8,128)(2,1)S(1)}, u32[]{:S(2)}) copy-start(bf16[256,512]{1,0:T(8,128)(2,1)S(1)} %collective-permute-done.6.refs_5_) | copy-start | bytes 786436
  28.0 7.0 %collective-permute-start.20 = (bf16[256,512]{1,0:T(8,128)(2,1)S(1)}, bf16[256,512]{1,0:T(8,128)(2,1)S(1)}, u32[]{:S(2)}, u32[]{:S(2)}) collective-permute-start(bf16[256,512]{1,0:T(8,128)(2,1)S(1)} %collective-permute-done.2.refs_2_), channel_id=1, source_target_pairs={{0,2},{2,0},{4,6},{6,4},{8,10},{10,8},{12,14},{14,12},{16,18},{18,... | collective-permute-start | bytes 786440 | tf_op jit(solution)/shard_map/ppermute | solution.py:290
  29.4 34.8 %copy-start.5 = (bf16[256,512]{1,0:T(8,128)(2,1)}, bf16[256,512]{1,0:T(8,128)(2,1)S(1)}, u32[]{:S(2)}) copy-start(bf16[256,512]{1,0:T(8,128)(2,1)S(1)} %collective-permute-done.1.refs_1_) | copy-start | bytes 786436
  29.4 11.8 %collective-permute-start.11 = (bf16[256,512]{1,0:T(8,128)(2,1)S(1)}, bf16[256,512]{1,0:T(8,128)(2,1)S(1)}, u32[]{:S(2)}, u32[]{:S(2)}) collective-permute-start(bf16[256,512]{1,0:T(8,128)(2,1)S(1)} %collective-permute-done.2.refs_2_), channel_id=1, source_target_pairs={{0,12},{2,14},{4,8},{6,10},{8,4},{10,6},{12,0},{14,2},{16,28},{18,... | collective-permute-start | bytes 786440 | tf_op jit(solution)/shard_map/ppermute | solution.py:290
  35.0 15.1 %collective-permute-start.7 = (bf16[256,512]{1,0:T(8,128)(2,1)S(1)}, bf16[256,512]{1,0:T(8,128)(2,1)S(1)}, u32[]{:S(2)}, u32[]{:S(2)}) collective-permute-start(bf16[256,512]{1,0:T(8,128)(2,1)S(1)} %collective-permute-done.2.refs_2_), channel_id=1, source_target_pairs={{0,8},{2,10},{4,12},{6,14},{8,0},{10,2},{12,4},{14,6},{16,24},{18,... | collective-permute-start | bytes 786440 | tf_op jit(solution)/shard_map/ppermute | solution.py:290
  35.0 16.8 %copy-start.9 = (bf16[256,512]{1,0:T(8,128)(2,1)}, bf16[256,512]{1,0:T(8,128)(2,1)S(1)}, u32[]{:S(2)}) copy-start(bf16[256,512]{1,0:T(8,128)(2,1)S(1)} %collective-permute-done.20.refs_4_) | copy-start | bytes 786436
  35.0 15.7 %collective-permute-start.3 = (bf16[256,512]{1,0:T(8,128)(2,1)S(1)}, bf16[256,512]{1,0:T(8,128)(2,1)S(1)}, u32[]{:S(2)}, u32[]{:S(2)}) collective-permute-start(bf16[256,512]{1,0:T(8,128)(2,1)S(1)} %collective-permute-done.2.refs_2_), channel_id=1, source_target_pairs={{0,4},{2,6},{4,0},{6,2},{8,12},{10,14},{12,8},{14,10},{16,20},{18,... | collective-permute-start | bytes 786440 | tf_op jit(solution)/shard_map/ppermute | solution.py:290
  41.2 23.0 %copy-start.8 = (bf16[256,512]{1,0:T(8,128)(2,1)}, bf16[256,512]{1,0:T(8,128)(2,1)S(1)}, u32[]{:S(2)}) copy-start(bf16[256,512]{1,0:T(8,128)(2,1)S(1)} %collective-permute-done.11.refs_10_) | copy-start | bytes 786436
  41.2 9.6 %collective-permute-start.10 = (bf16[256,512]{1,0:T(8,128)(2,1)S(1)}, bf16[256,512]{1,0:T(8,128)(2,1)S(1)}, u32[]{:S(2)}, u32[]{:S(2)}) collective-permute-start(bf16[256,512]{1,0:T(8,128)(2,1)S(1)} %collective-permute-done.6.refs_5_), channel_id=1, source_target_pairs={{0,4},{2,6},{4,0},{6,2},{8,12},{10,14},{12,8},{14,10},{16,20},{18,... | collective-permute-start | bytes 786440 | tf_op jit(solution)/shard_map/ppermute | solution.py:290
  42.0 9.3 %collective-permute-start.8 = (bf16[256,512]{1,0:T(8,128)(2,1)S(1)}, bf16[256,512]{1,0:T(8,128)(2,1)S(1)}, u32[]{:S(2)}, u32[]{:S(2)}) collective-permute-start(bf16[256,512]{1,0:T(8,128)(2,1)S(1)} %collective-permute-done.6.refs_5_), channel_id=1, source_target_pairs={{0,2},{2,0},{4,6},{6,4},{8,10},{10,8},{12,14},{14,12},{16,18},{18,... | collective-permute-start | bytes 786440 | tf_op jit(solution)/shard_map/ppermute | solution.py:290
  50.1 14.1 %copy-start.10 = (bf16[256,512]{1,0:T(8,128)(2,1)}, bf16[256,512]{1,0:T(8,128)(2,1)S(1)}, u32[]{:S(2)}) copy-start(bf16[256,512]{1,0:T(8,128)(2,1)S(1)} %collective-permute-done.7.refs_6_) | copy-start | bytes 786436
  50.1 14.2 %collective-permute-start.4 = (bf16[256,512]{1,0:T(8,128)(2,1)S(1)}, bf16[256,512]{1,0:T(8,128)(2,1)S(1)}, u32[]{:S(2)}, u32[]{:S(2)}) collective-permute-start(bf16[256,512]{1,0:T(8,128)(2,1)S(1)} %collective-permute-done.1.refs_1_), channel_id=1, source_target_pairs={{0,2},{2,0},{4,6},{6,4},{8,10},{10,8},{12,14},{14,12},{16,18},{18,... | collective-permute-start | bytes 786440 | tf_op jit(solution)/shard_map/ppermute | solution.py:290
  50.7 13.5 %copy-start.11 = (bf16[256,512]{1,0:T(8,128)(2,1)}, bf16[256,512]{1,0:T(8,128)(2,1)S(1)}, u32[]{:S(2)}) copy-start(bf16[256,512]{1,0:T(8,128)(2,1)S(1)} %collective-permute-done.3.refs_2_) | copy-start | bytes 786436
  50.7 13.6 %collective-permute-start.13 = (bf16[256,512]{1,0:T(8,128)(2,1)S(1)}, bf16[256,512]{1,0:T(8,128)(2,1)S(1)}, u32[]{:S(2)}, u32[]{:S(2)}) collective-permute-start(bf16[256,512]{1,0:T(8,128)(2,1)S(1)} %collective-permute-done.11.refs_10_), channel_id=1, source_target_pairs={{0,2},{2,0},{4,6},{6,4},{8,10},{10,8},{12,14},{14,12},{16,18},{18,... | collective-permute-start | bytes 786440 | tf_op jit(solution)/shard_map/ppermute | solution.py:290
  50.8 13.4 %copy-start.12 = (bf16[256,512]{1,0:T(8,128)(2,1)}, bf16[256,512]{1,0:T(8,128)(2,1)S(1)}, u32[]{:S(2)}) copy-start(bf16[256,512]{1,0:T(8,128)(2,1)S(1)} %collective-permute-done.10.refs_9_) | copy-start | bytes 786436
  50.8 13.5 %collective-permute-start.9 = (bf16[256,512]{1,0:T(8,128)(2,1)S(1)}, bf16[256,512]{1,0:T(8,128)(2,1)S(1)}, u32[]{:S(2)}, u32[]{:S(2)}) collective-permute-start(bf16[256,512]{1,0:T(8,128)(2,1)S(1)} %collective-permute-done.7.refs_6_), channel_id=1, source_target_pairs={{0,2},{2,0},{4,6},{6,4},{8,10},{10,8},{12,14},{14,12},{16,18},{18,... | collective-permute-start | bytes 786440 | tf_op jit(solution)/shard_map/ppermute | solution.py:290
  51.2 13.0 %copy-start.13 = (bf16[256,512]{1,0:T(8,128)(2,1)}, bf16[256,512]{1,0:T(8,128)(2,1)S(1)}, u32[]{:S(2)}) copy-start(bf16[256,512]{1,0:T(8,128)(2,1)S(1)} %collective-permute-done.8.refs_7_) | copy-start | bytes 786436
  51.3 13.1 %collective-permute-start.5 = (bf16[256,512]{1,0:T(8,128)(2,1)S(1)}, bf16[256,512]{1,0:T(8,128)(2,1)}, u32[]{:S(2)}, u32[]{:S(2)}) collective-permute-start(bf16[256,512]{1,0:T(8,128)(2,1)S(1)} %collective-permute-done.3.refs_2_), channel_id=1, source_target_pairs={{0,2},{2,0},{4,6},{6,4},{8,10},{10,8},{12,14},{14,12},{16,18},{18,... | collective-permute-start | bytes 786440 | tf_op jit(solution)/shard_map/ppermute | solution.py:290
  51.3 13.0 %collective-permute-start.12 = (bf16[256,512]{1,0:T(8,128)(2,1)S(1)}, bf16[256,512]{1,0:T(8,128)(2,1)}, u32[]{:S(2)}, u32[]{:S(2)}) collective-permute-start(bf16[256,512]{1,0:T(8,128)(2,1)S(1)} %collective-permute-done.10.refs_9_), channel_id=1, source_target_pairs={{0,2},{2,0},{4,6},{6,4},{8,10},{10,8},{12,14},{14,12},{16,18},{18,... | collective-permute-start | bytes 786440 | tf_op jit(solution)/shard_map/ppermute | solution.py:290
  64.3 0.9 copy-start.14
  64.3 0.7 copy-start.15
  64.3 0.8 copy-start.16
  65.2 33.1 %copy-start.2 = (bf16[1,1024,512]{2,1,0:T(8,128)(2,1)S(1)}, bf16[1,1024,512]{2,1,0:T(8,128)(2,1)}, u32[]{:S(2)}) copy-start(bf16[1,1024,512]{2,1,0:T(8,128)(2,1)} %get-tuple-element.30.n_own_ref) | copy-start | bytes 3145732
  98.1 14.9 %collective-permute-start.21 = (bf16[3,1024,512]{2,1,0:T(8,128)(2,1)}, bf16[3,1024,512]{2,1,0:T(8,128)(2,1)S(1)}, u32[]{:S(2)}, u32[]{:S(2)}) collective-permute-start(bf16[3,1024,512]{2,1,0:T(8,128)(2,1)} %get-tuple-element.29.n_own_ref), channel_id=1, source_target_pairs={{0,2},{2,0},{4,6},{6,4},{8,10},{10,8},{12,14},{14,12},{16,18},{18,... | collective-permute-start | bytes 9437192 | tf_op jit(solution)/shard_map/ppermute | solution.py:290
  98.3 7.2 %collective-permute-start.22 = (bf16[1,1024,512]{2,1,0:T(8,128)(2,1)S(1)}, bf16[1,1024,512]{2,1,0:T(8,128)(2,1)S(1)}, u32[]{:S(2)}, u32[]{:S(2)}) collective-permute-start(bf16[1,1024,512]{2,1,0:T(8,128)(2,1)S(1)} %copy-done.2), channel_id=1, source_target_pairs={{0,2},{2,0},{4,6},{6,4},{8,10},{10,8},{12,14},{14,12},{16,18},{18,... | collective-permute-start | bytes 3145736 | tf_op jit(solution)/shard_map/ppermute | solution.py:290
  105.5 1.0 copy-start.3
  113.0 1.8 %copy-start = (bf16[3,1024,512]{2,1,0:T(8,128)(2,1)}, bf16[3,1024,512]{2,1,0:T(8,128)(2,1)S(1)}, u32[]{:S(2)}) copy-start(bf16[3,1024,512]{2,1,0:T(8,128)(2,1)S(1)} %collective-permute-done.21.n_other_ref) | copy-start | bytes 9437188
where the time goes:
time: 127 us; the launch traced here: 126 us
  Pallas kernels  71 us (56%)
  waiting for transfers between devices  24.9 us (20%)
  starting transfers between devices  23.9 us (19%)
  local copies, waits for them, and re-layouts  3.6 us (3%)
  other arithmetic  2.2 us (2%)
    pallas_call x2, Pallas kernels, step_blocks(): pl.pallas_call(kernel, grid_spec=pltpu.PrefetchScalarGridSpec(num_scalar_...  45.3 us
    ppermute x21, waiting for transfers between devices, hop(): return lax.ppermute(array, 'col', [(i, i ^ mask) for i in range(size)])  24.1 us
    ppermute x21, starting transfers between devices, hop(): return lax.ppermute(array, 'col', [(i, i ^ mask) for i in range(size)])  20.8 us
    pallas_call x2, Pallas kernels, update_blocks(): pl.pallas_call(functools.partial(update_kernel, len(carried)), grid_spec=...  18.2 us
    pallas_call x1, Pallas kernels, early(): pl.pallas_call(early_kernel, grid_spec=pltpu.PrefetchScalarGridSpec(num_s...  7.48 us
    unnamed x38, local copies, waits for them, and re-layouts  3.6 us
    ppermute x2, starting transfers between devices, across(): return lax.ppermute(array, 'tok', [(0, 1), (1, 0)])  3.1 us
  transfers between devices with their start and end apart: 23, of which 6 were waited for; matrix products, arithmetic and copies ran while one was open for 2% of the time, Pallas kernels for 21%

commit v1 on v0

--- a/solution.py
+++ b/solution.py
@@ -107,23 +107,25 @@
         full_ref[tokens:, away] = h1_ref[...]
         gram_ref[...] = dot(full_ref[...], full_ref[...], 1, 1).astype(bf16)
 
-    x = dot(full_ref[:, at], right_own_ref[0], 1, 0) + dot(full_ref[:, away], right_other_ref[0], 1, 0)
-    x_ref[0] = x.astype(bf16)
+    for j in range(x_ref.shape[0]):
+        x = dot(full_ref[:, at], right_own_ref[j], 1, 0) + dot(full_ref[:, away], right_other_ref[j], 1, 0)
+        x_ref[j] = x.astype(bf16)
 
 
 def early(half, grads, right_own, right_other):
     blocks, width, order = right_own.shape
     tokens = 2 * grads[0].shape[0]
     whole = lambda n, s: (0, 0)
-    column = pl.BlockSpec((1, width, width), lambda n, s: (n, 0, s[0]))
+    many = 2
+    column = pl.BlockSpec((many, width, width), lambda n, s: (n, 0, s[0]))
     return pl.pallas_call(
         early_kernel,
         grid_spec=pltpu.PrefetchScalarGridSpec(
             num_scalar_prefetch=1,
-            grid=(blocks,),
+            grid=(blocks // many,),
             in_specs=[pl.BlockSpec((tokens // 2, width), whole)] * 4 + [column, column],
             out_specs=[
-                pl.BlockSpec((1, tokens, width), lambda n, s: (n, 0, 0)),
+                pl.BlockSpec((many, tokens, width), lambda n, s: (n, 0, 0)),
                 pl.BlockSpec((tokens, order), whole),
                 pl.BlockSpec((tokens, tokens), whole),
             ],
@@ -269,7 +271,7 @@
         ),
         out_shape=jax.ShapeDtypeStruct((blocks, order, width), bf16),
         input_output_aliases={7: 0} if carried else {},
-        compiler_params=pltpu.CompilerParams(vmem_limit_bytes=56 << 20),
+        compiler_params=pltpu.CompilerParams(vmem_limit_bytes=32 << 20),
         cost_estimate=pl.CostEstimate(
             flops=8 * count * unit, bytes_accessed=count * 8 * order * width, transcendentals=0
         ),

time: 127 us -> 125 us (0.984)
  Pallas kernels: 71 us -> 67.7 us
  local copies, waits for them, and re-layouts: 3.6 us -> 5.28 us
    pallas_call x2, Pallas kernels: 18.2 us -> 15.5 us  [update_blocks(): pl.pallas_call(functools.partial(update_kernel, len(carried)), grid_spec=...]
    unnamed x38 -> x50, local copies, waits for them, and re-layouts: 3.6 us -> 5.28 us
  transfers between devices with their start and end apart: 23 -> 23, of which waited for: 6 -> 6; matrix products, arithmetic and copies ran while one was open for 2% -> 2% of each run, Pallas kernels for 21% -> 20%
where the time goes in v1:
time: 125 us
  Pallas kernels  67.7 us (54%)
  waiting for transfers between devices  24.8 us (20%)
  starting transfers between devices  23.9 us (19%)
  local copies, waits for them, and re-layouts  5.28 us (4%)
  other arithmetic  2.21 us (2%)
    pallas_call x2, Pallas kernels, step_blocks(): pl.pallas_call(kernel, grid_spec=pltpu.PrefetchScalarGridSpec(num_scalar_...  45.3 us
    ppermute x21, waiting for transfers between devices, hop(): return lax.ppermute(array, 'col', [(i, i ^ mask) for i in range(size)])  24 us
    ppermute x21, starting transfers between devices, hop(): return lax.ppermute(array, 'col', [(i, i ^ mask) for i in range(size)])  20.8 us
    pallas_call x2, Pallas kernels, update_blocks(): pl.pallas_call(functools.partial(update_kernel, len(carried)), grid_spec=...  15.5 us
    pallas_call x1, Pallas kernels, early(): pl.pallas_call(early_kernel, grid_spec=pltpu.PrefetchScalarGridSpec(num_s...  6.86 us
    unnamed x50, local copies, waits for them, and re-layouts  5.28 us
    ppermute x2, starting transfers between devices, across(): return lax.ppermute(array, 'tok', [(0, 1), (1, 0)])  3.1 us
  transfers between devices with their start and end apart: 23, of which 6 were waited for; matrix products, arithmetic and copies ran while one was open for 2% of the time, Pallas kernels for 20%

profile of v1, /device:TPU:0, one launch (start us, length us, event | category | flops | bytes accessed | tf_op | source)
XLA Modules:
  0.0 124.8 jit_solution(11355143405229294875)
XLA Ops:
  0.6 0.6 collective-permute-start.17
  1.2 0.1 collective-permute-start.18
  1.3 5.0 %collective-permute-start = (bf16[256,512]{1,0:T(8,128)(2,1)}, bf16[256,512]{1,0:T(8,128)(2,1)S(1)}, u32[]{:S(2)}, u32[]{:S(2)}) collective-permute-start(bf16[256,512]{1,0:T(8,128)(2,1)} %param.8), channel_id=1, source_target_pairs={{0,24},{2,26},{4,28},{6,30},{8,16},{10,18},{12,20},{14,22},{16,8},... | collective-permute-start | bytes 786440 | tf_op jit(solution)/shard_map/ppermute | solution.py:292
  6.3 1.5 %collective-permute-start.14 = (bf16[256,512]{1,0:T(8,128)(2,1)}, bf16[256,512]{1,0:T(8,128)(2,1)S(1)}, u32[]{:S(2)}, u32[]{:S(2)}) collective-permute-start(bf16[256,512]{1,0:T(8,128)(2,1)} %g0_ref.1), channel_id=1, source_target_pairs={{0,1},{1,0},{2,3},{3,2},{4,5},{5,4},{6,7},{7,6},{8,9},{9,8},{10,11... | collective-permute-start | bytes 786440 | tf_op jit(solution)/shard_map/ppermute | solution.py:295
  7.8 5.3 %collective-permute-done = bf16[256,512]{1,0:T(8,128)(2,1)S(1)} collective-permute-done((bf16[256,512]{1,0:T(8,128)(2,1)}, bf16[256,512]{1,0:T(8,128)(2,1)S(1)}, u32[]{:S(2)}, u32[]{:S(2)}) %collective-permute-start) | collective-permute-done | bytes 262176 | tf_op jit(solution)/shard_map/ppermute | solution.py:292
  13.1 1.0 broadcast_select_fusion
  14.1 1.6 %collective-permute-start.2 = (bf16[256,512]{1,0:T(8,128)(2,1)S(1)}, bf16[256,512]{1,0:T(8,128)(2,1)S(1)}, u32[]{:S(2)}, u32[]{:S(2)}) collective-permute-start(bf16[256,512]{1,0:T(8,128)(2,1)S(1)} %get-tuple-element.31), channel_id=1, source_target_pairs={{0,1},{1,0},{2,3},{3,2},{4,5},{5,4},{6,7},{7,6},{8,9},{9,8},{10,11... | collective-permute-start | bytes 786440 | tf_op jit(solution)/shard_map/ppermute | solution.py:295
  15.7 0.0 collective-permute-done.15.h0_ref
  15.8 0.0 copy-start.23
  15.8 5.3 %collective-permute-start.6 = (bf16[256,512]{1,0:T(8,128)(2,1)S(1)}, bf16[256,512]{1,0:T(8,128)(2,1)S(1)}, u32[]{:S(2)}, u32[]{:S(2)}) collective-permute-start(bf16[256,512]{1,0:T(8,128)(2,1)S(1)} %get-tuple-element.32.refs_1_), channel_id=1, source_target_pairs={{0,8},{2,10},{4,12},{6,14},{8,0},{10,2},{12,4},{14,6},{16,24},{18,... | collective-permute-start | bytes 786440 | tf_op jit(solution)/shard_map/ppermute | solution.py:292
  21.1 0.8 collective-permute-done.2.refs_2_
  21.9 1.3 %collective-permute-start.1 = (bf16[256,512]{1,0:T(8,128)(2,1)S(1)}, bf16[256,512]{1,0:T(8,128)(2,1)S(1)}, u32[]{:S(2)}, u32[]{:S(2)}) collective-permute-start(bf16[256,512]{1,0:T(8,128)(2,1)S(1)} %get-tuple-element.32.refs_1_), channel_id=1, source_target_pairs={{0,4},{2,6},{4,0},{6,2},{8,12},{10,14},{12,8},{14,10},{16,20},{18,... | collective-permute-start | bytes 786440 | tf_op jit(solution)/shard_map/ppermute | solution.py:292
  23.2 0.0 collective-permute-start.16
  23.2 4.8 %collective-permute-done.6.refs_5_ = bf16[256,512]{1,0:T(8,128)(2,1)S(1)} collective-permute-done((bf16[256,512]{1,0:T(8,128)(2,1)S(1)}, bf16[256,512]{1,0:T(8,128)(2,1)S(1)}, u32[]{:S(2)}, u32[]{:S(2)}) %collective-permute-start.6) | collective-permute-done | bytes 262176 | tf_op jit(solution)/shard_map/ppermute | solution.py:292
  28.0 0.0 collective-permute-start.20
  28.0 1.5 %collective-permute-done.1.refs_1_ = bf16[256,512]{1,0:T(8,128)(2,1)S(1)} collective-permute-done((bf16[256,512]{1,0:T(8,128)(2,1)S(1)}, bf16[256,512]{1,0:T(8,128)(2,1)S(1)}, u32[]{:S(2)}, u32[]{:S(2)}) %collective-permute-start.1) | collective-permute-done | bytes 262176 | tf_op jit(solution)/shard_map/ppermute | solution.py:292
  29.4 5.0 %collective-permute-start.11 = (bf16[256,512]{1,0:T(8,128)(2,1)S(1)}, bf16[256,512]{1,0:T(8,128)(2,1)S(1)}, u32[]{:S(2)}, u32[]{:S(2)}) collective-permute-start(bf16[256,512]{1,0:T(8,128)(2,1)S(1)} %collective-permute-done.2.refs_2_), channel_id=1, source_target_pairs={{0,12},{2,14},{4,8},{6,10},{8,4},{10,6},{12,0},{14,2},{16,28},{18,... | collective-permute-start | bytes 786440 | tf_op jit(solution)/shard_map/ppermute | solution.py:292
  34.4 0.7 pad_add_fusion.1.half_ref.refs_0_.scal_ref
  35.1 0.0 collective-permute-done.20.refs_4_
  35.1 0.6 collective-permute-start.3
  35.7 5.5 %collective-permute-done.11.refs_10_ = bf16[256,512]{1,0:T(8,128)(2,1)S(1)} collective-permute-done((bf16[256,512]{1,0:T(8,128)(2,1)S(1)}, bf16[256,512]{1,0:T(8,128)(2,1)S(1)}, u32[]{:S(2)}, u32[]{:S(2)}) %collective-permute-start.11) | collective-permute-done | bytes 262176 | tf_op jit(solution)/shard_map/ppermute | solution.py:292
  41.2 0.8 collective-permute-start.10
  42.0 0.6 pad_add_fusion.refs_0_.scal_ref
  42.6 6.9 %early.1 = (bf16[4,512,512]{2,1,0:T(8,128)(2,1)}, bf16[512,1024]{1,0:T(8,128)(2,1)}, bf16[512,512]{1,0:T(8,128)(2,1)}) custom-call(s32[2]{0:T(128)} %pad_add_fusion.1.half_ref.refs_0_.scal_ref, bf16[256,512]{1,0:T(8,128)(2,1)} %g0_ref.1, bf16[256,512]{1,0:T(8,128)(2,1)} %copy-done.22, bf16[256,512]{1,0:T(8,128)(2,1)} %copy-done.23, ...), custom_call_target="tpu_custom_call" | custom-call | flops 2684354560 | bytes 8388608 | tf_op jit(solution)/shard_map/early/pallas_call | solution.py:121
  49.5 0.0 collective-permute-done.7.refs_6_
  49.5 0.6 collective-permute-start.4
  50.0 0.0 collective-permute-done.3.refs_2_
  50.0 0.1 collective-permute-start.13
  50.1 0.4 collective-permute-start.9
  50.6 0.1 collective-permute-start.5
  50.7 0.0 collective-permute-done.18.refs_9_.refs_17_.ql_other_ref
  50.7 0.4 collective-permute-start.12
  51.1 12.4 %step.2 = (f32[4,512,1024]{2,1,0:T(8,128)}, f32[4,512,1024]{2,1,0:T(8,128)}, f32[4,1024,512]{2,1,0:T(8,128)}, f32[4,1024,512]{2,1,0:T(8,128)}, bf16[1,1024,512]{2,1,0:T(8,128)(2,1)}) custom-call(s32[2]{0:T(128)} %pad_add_fusion.1.half_ref.refs_0_.scal_ref, bf16[256,512]{1,0:T(8,128)(2,1)} %copy-done.8, bf16[256,512]{1,0:T(8,128)(2,1)} %copy-done.11, ...), custom_call_target="tpu_custom_call" | custom-call | flops 3758096384 | bytes 9437184 | tf_op jit(solution)/shard_map/step/pallas_call | solution.py:211
  63.6 0.0 collective-permute-done.4.refs_3_
  63.6 0.0 collective-permute-done.13.refs_12_
  63.6 0.0 collective-permute-done.5.refs_4_
  63.6 0.0 collective-permute-done.12.refs_11_
  63.7 0.7 copy-done.21
  64.4 0.1 copy-done.20
  64.5 32.9 %step.3 = (f32[4,512,1024]{2,1,0:T(8,128)}, f32[4,512,1024]{2,1,0:T(8,128)}, f32[4,1024,512]{2,1,0:T(8,128)}, f32[4,1024,512]{2,1,0:T(8,128)}, bf16[3,1024,512]{2,1,0:T(8,128)(2,1)}) custom-call(s32[4]{0:T(128)} %pad_add_fusion.refs_0_.scal_ref, ...), custom_call_target="tpu_custom_call", output_to_operand_aliasing={{0}: (22, {}), {1}: (23, {}), {2}: (24, {}), {3}: (25, {})} | custom-call | flops 11274289152 | bytes 28311552 | tf_op jit(solution)/shard_map/step/pallas_call | solution.py:211
  97.4 0.2 collective-permute-start.21
  97.6 0.4 collective-permute-start.22
  98.0 6.9 %collective-permute-done.22.n_other_ref = bf16[1,1024,512]{2,1,0:T(8,128)(2,1)S(1)} collective-permute-done((bf16[1,1024,512]{2,1,0:T(8,128)(2,1)S(1)}, bf16[1,1024,512]{2,1,0:T(8,128)(2,1)S(1)}, u32[]{:S(2)}, u32[]{:S(2)}) %collective-permute-start.22) | collective-permute-done | bytes 1048608 | tf_op jit(solution)/shard_map/ppermute | solution.py:292
  104.8 2.2 %copy-done = bf16[4,512,1024]{2,1,0:T(8,128)(2,1)S(1)} copy-done((bf16[4,512,1024]{2,1,0:T(8,128)(2,1)S(1)}, bf16[4,512,1024]{2,1,0:T(8,128)(2,1)}, u32[]{:S(2)}) %copy-start) | copy-done | bytes 4194328
  107.0 2.2 %copy-done.2 = bf16[4,512,1024]{2,1,0:T(8,128)(2,1)S(1)} copy-done((bf16[4,512,1024]{2,1,0:T(8,128)(2,1)S(1)}, bf16[4,512,1024]{2,1,0:T(8,128)(2,1)}, u32[]{:S(2)}) %copy-start.2) | copy-done | bytes 4194328
  109.2 5.5 %update.2.rest_0_ = bf16[4,1024,512]{2,1,0:T(8,128)(2,1)} custom-call(s32[2]{0:T(128)S(1)} %copy-done.7, bf16[1,1024,512]{2,1,0:T(8,128)(2,1)S(1)} %copy-done.5, bf16[1,1024,512]{2,1,0:T(8,128)(2,1)S(1)} %collective-permute-done.22.n_other_ref, bf16[4,512,1024]{2,1,0:T(8,128)(2,1)S(1)} %copy-done, bf16[4,512,1024]{2,1,0:T(8,128)(2,1)S(1)} %copy-done, ...), custom_call_target="tpu_custom_call" | custom-call | flops 2147483648 | bytes 4194304 | tf_op jit(solution)/shard_map/update/pallas_call | solution.py:255
  114.7 0.0 collective-permute-done.21.n_other_ref
  114.7 10.1 %update.3 = bf16[4,1024,512]{2,1,0:T(8,128)(2,1)} custom-call(s32[4]{0:T(128)S(1)} %copy-done.6, bf16[3,1024,512]{2,1,0:T(8,128)(2,1)S(1)} %copy-done.4, bf16[3,1024,512]{2,1,0:T(8,128)(2,1)S(1)} %collective-permute-done.21.n_other_ref, bf16[4,512,1024]{2,1,0:T(8,128)(2,1)S(1)} %copy-done.1, ...), custom_call_target="tpu_custom_call", output_to_operand_aliasing={{}: (7, {})} | custom-call | flops 6442450944 | bytes 12582912 | tf_op jit(solution)/shard_map/update/pallas_call | solution.py:255
  (56 shorter events, 0.1 us)
Async XLA Ops:
  0.6 41.4 %collective-permute-start.17 = (bf16[4,512,1024]{2,1,0:T(8,128)(2,1)}, bf16[4,512,1024]{2,1,0:T(8,128)(2,1)}, u32[]{:S(2)}, u32[]{:S(2)}) collective-permute-start(bf16[4,512,1024]{2,1,0:T(8,128)(2,1)} %q_other_ref.3), channel_id=1, source_target_pairs={{0,2},{2,0},{4,6},{6,4},{8,10},{10,8},{12,14},{14,12},{16,18},{18,... | collective-permute-start | bytes 12582920 | tf_op jit(solution)/shard_map/ppermute | solution.py:292
  1.2 49.5 %collective-permute-start.18 = (bf16[4,512,1024]{2,1,0:T(8,128)(2,1)}, bf16[4,512,1024]{2,1,0:T(8,128)(2,1)}, u32[]{:S(2)}, u32[]{:S(2)}) collective-permute-start(bf16[4,512,1024]{2,1,0:T(8,128)(2,1)} %ql_own_ref.3), channel_id=1, source_target_pairs={{0,2},{2,0},{4,6},{6,4},{8,10},{10,8},{12,14},{14,12},{16,18},{18,... | collective-permute-start | bytes 12582920 | tf_op jit(solution)/shard_map/ppermute | solution.py:292
  1.3 11.9 %collective-permute-start = (bf16[256,512]{1,0:T(8,128)(2,1)}, bf16[256,512]{1,0:T(8,128)(2,1)S(1)}, u32[]{:S(2)}, u32[]{:S(2)}) collective-permute-start(bf16[256,512]{1,0:T(8,128)(2,1)} %param.8), channel_id=1, source_target_pairs={{0,24},{2,26},{4,28},{6,30},{8,16},{10,18},{12,20},{14,22},{16,8},... | collective-permute-start | bytes 786440 | tf_op jit(solution)/shard_map/ppermute | solution.py:292
  6.3 9.5 %collective-permute-start.14 = (bf16[256,512]{1,0:T(8,128)(2,1)}, bf16[256,512]{1,0:T(8,128)(2,1)S(1)}, u32[]{:S(2)}, u32[]{:S(2)}) collective-permute-start(bf16[256,512]{1,0:T(8,128)(2,1)} %g0_ref.1), channel_id=1, source_target_pairs={{0,1},{1,0},{2,3},{3,2},{4,5},{5,4},{6,7},{7,6},{8,9},{9,8},{10,11... | collective-permute-start | bytes 786440 | tf_op jit(solution)/shard_map/ppermute | solution.py:295
  7.8 7.9 %collective-permute-start.15 = (bf16[256,512]{1,0:T(8,128)(2,1)}, bf16[256,512]{1,0:T(8,128)(2,1)S(1)}, u32[]{:S(2)}, u32[]{:S(2)}) collective-permute-start(bf16[256,512]{1,0:T(8,128)(2,1)} %g0_ref.1), channel_id=1, source_target_pairs={{0,2},{2,0},{4,6},{6,4},{8,10},{10,8},{12,14},{14,12},{16,18},{18,... | collective-permute-start | bytes 786440 | tf_op jit(solution)/shard_map/ppermute | solution.py:292
  14.1 36.9 %copy-start.8 = (bf16[256,512]{1,0:T(8,128)(2,1)}, bf16[256,512]{1,0:T(8,128)(2,1)S(1)}, u32[]{:S(2)}) copy-start(bf16[256,512]{1,0:T(8,128)(2,1)S(1)} %get-tuple-element.32.refs_1_) | copy-start | bytes 786436
  14.1 7.7 %collective-permute-start.2 = (bf16[256,512]{1,0:T(8,128)(2,1)S(1)}, bf16[256,512]{1,0:T(8,128)(2,1)S(1)}, u32[]{:S(2)}, u32[]{:S(2)}) collective-permute-start(bf16[256,512]{1,0:T(8,128)(2,1)S(1)} %get-tuple-element.31), channel_id=1, source_target_pairs={{0,1},{1,0},{2,3},{3,2},{4,5},{5,4},{6,7},{7,6},{8,9},{9,8},{10,11... | collective-permute-start | bytes 786440 | tf_op jit(solution)/shard_map/ppermute | solution.py:295
  15.7 26.8 %copy-start.22 = (bf16[256,512]{1,0:T(8,128)(2,1)}, bf16[256,512]{1,0:T(8,128)(2,1)S(1)}, u32[]{:S(2)}) copy-start(bf16[256,512]{1,0:T(8,128)(2,1)S(1)} %collective-permute-done.14.g1_ref) | copy-start | bytes 786436
  15.7 7.4 %collective-permute-start.19 = (bf16[256,512]{1,0:T(8,128)(2,1)S(1)}, bf16[256,512]{1,0:T(8,128)(2,1)S(1)}, u32[]{:S(2)}, u32[]{:S(2)}) collective-permute-start(bf16[256,512]{1,0:T(8,128)(2,1)S(1)} %get-tuple-element.32.refs_1_), channel_id=1, source_target_pairs={{0,2},{2,0},{4,6},{6,4},{8,10},{10,8},{12,14},{14,12},{16,18},{18,... | collective-permute-start | bytes 786440 | tf_op jit(solution)/shard_map/ppermute | solution.py:292
  15.8 26.8 %copy-start.23 = (bf16[256,512]{1,0:T(8,128)(2,1)}, bf16[256,512]{1,0:T(8,128)(2,1)S(1)}, u32[]{:S(2)}) copy-start(bf16[256,512]{1,0:T(8,128)(2,1)S(1)} %collective-permute-done.15.h0_ref) | copy-start | bytes 786436
  15.8 12.2 %collective-permute-start.6 = (bf16[256,512]{1,0:T(8,128)(2,1)S(1)}, bf16[256,512]{1,0:T(8,128)(2,1)S(1)}, u32[]{:S(2)}, u32[]{:S(2)}) collective-permute-start(bf16[256,512]{1,0:T(8,128)(2,1)S(1)} %get-tuple-element.32.refs_1_), channel_id=1, source_target_pairs={{0,8},{2,10},{4,12},{6,14},{8,0},{10,2},{12,4},{14,6},{16,24},{18,... | collective-permute-start | bytes 786440 | tf_op jit(solution)/shard_map/ppermute | solution.py:292
  21.9 29.2 %copy-start.11 = (bf16[256,512]{1,0:T(8,128)(2,1)}, bf16[256,512]{1,0:T(8,128)(2,1)S(1)}, u32[]{:S(2)}) copy-start(bf16[256,512]{1,0:T(8,128)(2,1)S(1)} %collective-permute-done.2.refs_2_) | copy-start | bytes 786436
  21.9 7.5 %collective-permute-start.1 = (bf16[256,512]{1,0:T(8,128)(2,1)S(1)}, bf16[256,512]{1,0:T(8,128)(2,1)S(1)}, u32[]{:S(2)}, u32[]{:S(2)}) collective-permute-start(bf16[256,512]{1,0:T(8,128)(2,1)S(1)} %get-tuple-element.32.refs_1_), channel_id=1, source_target_pairs={{0,4},{2,6},{4,0},{6,2},{8,12},{10,14},{12,8},{14,10},{16,20},{18,... | collective-permute-start | bytes 786440 | tf_op jit(solution)/shard_map/ppermute | solution.py:292
  23.2 27.9 %copy-start.12 = (bf16[256,512]{1,0:T(8,128)(2,1)}, bf16[256,512]{1,0:T(8,128)(2,1)S(1)}, u32[]{:S(2)}) copy-start(bf16[256,512]{1,0:T(8,128)(2,1)S(1)} %collective-permute-done.19.refs_3_) | copy-start | bytes 786436
  23.2 11.9 %collective-permute-start.16 = (bf16[256,512]{1,0:T(8,128)(2,1)S(1)}, bf16[256,512]{1,0:T(8,128)(2,1)S(1)}, u32[]{:S(2)}, u32[]{:S(2)}) collective-permute-start(bf16[256,512]{1,0:T(8,128)(2,1)S(1)} %collective-permute-done.14.g1_ref), channel_id=1, source_target_pairs={{0,2},{2,0},{4,6},{6,4},{8,10},{10,8},{12,14},{14,12},{16,18},{18,... | collective-permute-start | bytes 786440 | tf_op jit(solution)/shard_map/ppermute | solution.py:292
  28.0 35.5 %copy-start.9 = (bf16[256,512]{1,0:T(8,128)(2,1)}, bf16[256,512]{1,0:T(8,128)(2,1)S(1)}, u32[]{:S(2)}) copy-start(bf16[256,512]{1,0:T(8,128)(2,1)S(1)} %collective-permute-done.6.refs_5_) | copy-start | bytes 786436
  28.0 7.1 %collective-permute-start.20 = (bf16[256,512]{1,0:T(8,128)(2,1)S(1)}, bf16[256,512]{1,0:T(8,128)(2,1)S(1)}, u32[]{:S(2)}, u32[]{:S(2)}) collective-permute-start(bf16[256,512]{1,0:T(8,128)(2,1)S(1)} %collective-permute-done.2.refs_2_), channel_id=1, source_target_pairs={{0,2},{2,0},{4,6},{6,4},{8,10},{10,8},{12,14},{14,12},{16,18},{18,... | collective-permute-start | bytes 786440 | tf_op jit(solution)/shard_map/ppermute | solution.py:292
  29.4 34.1 %copy-start.10 = (bf16[256,512]{1,0:T(8,128)(2,1)}, bf16[256,512]{1,0:T(8,128)(2,1)S(1)}, u32[]{:S(2)}) copy-start(bf16[256,512]{1,0:T(8,128)(2,1)S(1)} %collective-permute-done.1.refs_1_) | copy-start | bytes 786436
  29.4 11.8 %collective-permute-start.11 = (bf16[256,512]{1,0:T(8,128)(2,1)S(1)}, bf16[256,512]{1,0:T(8,128)(2,1)S(1)}, u32[]{:S(2)}, u32[]{:S(2)}) collective-permute-start(bf16[256,512]{1,0:T(8,128)(2,1)S(1)} %collective-permute-done.2.refs_2_), channel_id=1, source_target_pairs={{0,12},{2,14},{4,8},{6,10},{8,4},{10,6},{12,0},{14,2},{16,28},{18,... | collective-permute-start | bytes 786440 | tf_op jit(solution)/shard_map/ppermute | solution.py:292
  35.1 7.5 %copy-start.24 = (bf16[256,512]{1,0:T(8,128)(2,1)}, bf16[256,512]{1,0:T(8,128)(2,1)S(1)}, u32[]{:S(2)}) copy-start(bf16[256,512]{1,0:T(8,128)(2,1)S(1)} %collective-permute-done.16.h1_ref) | copy-start | bytes 786436
  35.1 14.4 %collective-permute-start.7 = (bf16[256,512]{1,0:T(8,128)(2,1)S(1)}, bf16[256,512]{1,0:T(8,128)(2,1)S(1)}, u32[]{:S(2)}, u32[]{:S(2)}) collective-permute-start(bf16[256,512]{1,0:T(8,128)(2,1)S(1)} %collective-permute-done.2.refs_2_), channel_id=1, source_target_pairs={{0,8},{2,10},{4,12},{6,14},{8,0},{10,2},{12,4},{14,6},{16,24},{18,... | collective-permute-start | bytes 786440 | tf_op jit(solution)/shard_map/ppermute | solution.py:292
  35.1 16.0 %copy-start.14 = (bf16[256,512]{1,0:T(8,128)(2,1)}, bf16[256,512]{1,0:T(8,128)(2,1)S(1)}, u32[]{:S(2)}) copy-start(bf16[256,512]{1,0:T(8,128)(2,1)S(1)} %collective-permute-done.20.refs_4_) | copy-start | bytes 786436
  35.1 14.9 %collective-permute-start.3 = (bf16[256,512]{1,0:T(8,128)(2,1)S(1)}, bf16[256,512]{1,0:T(8,128)(2,1)S(1)}, u32[]{:S(2)}, u32[]{:S(2)}) collective-permute-start(bf16[256,512]{1,0:T(8,128)(2,1)S(1)} %collective-permute-done.2.refs_2_), channel_id=1, source_target_pairs={{0,4},{2,6},{4,0},{6,2},{8,12},{10,14},{12,8},{14,10},{16,20},{18,... | collective-permute-start | bytes 786440 | tf_op jit(solution)/shard_map/ppermute | solution.py:292
  41.2 22.3 %copy-start.13 = (bf16[256,512]{1,0:T(8,128)(2,1)}, bf16[256,512]{1,0:T(8,128)(2,1)S(1)}, u32[]{:S(2)}) copy-start(bf16[256,512]{1,0:T(8,128)(2,1)S(1)} %collective-permute-done.11.refs_10_) | copy-start | bytes 786436
  41.2 8.9 %collective-permute-start.10 = (bf16[256,512]{1,0:T(8,128)(2,1)S(1)}, bf16[256,512]{1,0:T(8,128)(2,1)S(1)}, u32[]{:S(2)}, u32[]{:S(2)}) collective-permute-start(bf16[256,512]{1,0:T(8,128)(2,1)S(1)} %collective-permute-done.6.refs_5_), channel_id=1, source_target_pairs={{0,4},{2,6},{4,0},{6,2},{8,12},{10,14},{12,8},{14,10},{16,20},{18,... | collective-permute-start | bytes 786440 | tf_op jit(solution)/shard_map/ppermute | solution.py:292
  42.0 8.5 %collective-permute-start.8 = (bf16[256,512]{1,0:T(8,128)(2,1)S(1)}, bf16[256,512]{1,0:T(8,128)(2,1)S(1)}, u32[]{:S(2)}, u32[]{:S(2)}) collective-permute-start(bf16[256,512]{1,0:T(8,128)(2,1)S(1)} %collective-permute-done.6.refs_5_), channel_id=1, source_target_pairs={{0,2},{2,0},{4,6},{6,4},{8,10},{10,8},{12,14},{14,12},{16,18},{18,... | collective-permute-start | bytes 786440 | tf_op jit(solution)/shard_map/ppermute | solution.py:292
  49.5 14.1 %copy-start.15 = (bf16[256,512]{1,0:T(8,128)(2,1)}, bf16[256,512]{1,0:T(8,128)(2,1)S(1)}, u32[]{:S(2)}) copy-start(bf16[256,512]{1,0:T(8,128)(2,1)S(1)} %collective-permute-done.7.refs_6_) | copy-start | bytes 786436
  49.5 14.1 %collective-permute-start.4 = (bf16[256,512]{1,0:T(8,128)(2,1)S(1)}, bf16[256,512]{1,0:T(8,128)(2,1)S(1)}, u32[]{:S(2)}, u32[]{:S(2)}) collective-permute-start(bf16[256,512]{1,0:T(8,128)(2,1)S(1)} %collective-permute-done.1.refs_1_), channel_id=1, source_target_pairs={{0,2},{2,0},{4,6},{6,4},{8,10},{10,8},{12,14},{14,12},{16,18},{18,... | collective-permute-start | bytes 786440 | tf_op jit(solution)/shard_map/ppermute | solution.py:292
  50.0 13.5 %copy-start.16 = (bf16[256,512]{1,0:T(8,128)(2,1)}, bf16[256,512]{1,0:T(8,128)(2,1)S(1)}, u32[]{:S(2)}) copy-start(bf16[256,512]{1,0:T(8,128)(2,1)S(1)} %collective-permute-done.3.refs_2_) | copy-start | bytes 786436
  50.0 13.5 %collective-permute-start.13 = (bf16[256,512]{1,0:T(8,128)(2,1)S(1)}, bf16[256,512]{1,0:T(8,128)(2,1)S(1)}, u32[]{:S(2)}, u32[]{:S(2)}) collective-permute-start(bf16[256,512]{1,0:T(8,128)(2,1)S(1)} %collective-permute-done.11.refs_10_), channel_id=1, source_target_pairs={{0,2},{2,0},{4,6},{6,4},{8,10},{10,8},{12,14},{14,12},{16,18},{18,... | collective-permute-start | bytes 786440 | tf_op jit(solution)/shard_map/ppermute | solution.py:292
  50.1 13.4 %copy-start.17 = (bf16[256,512]{1,0:T(8,128)(2,1)}, bf16[256,512]{1,0:T(8,128)(2,1)S(1)}, u32[]{:S(2)}) copy-start(bf16[256,512]{1,0:T(8,128)(2,1)S(1)} %collective-permute-done.10.refs_9_) | copy-start | bytes 786436
  50.1 13.5 %collective-permute-start.9 = (bf16[256,512]{1,0:T(8,128)(2,1)S(1)}, bf16[256,512]{1,0:T(8,128)(2,1)S(1)}, u32[]{:S(2)}, u32[]{:S(2)}) collective-permute-start(bf16[256,512]{1,0:T(8,128)(2,1)S(1)} %collective-permute-done.7.refs_6_), channel_id=1, source_target_pairs={{0,2},{2,0},{4,6},{6,4},{8,10},{10,8},{12,14},{14,12},{16,18},{18,... | collective-permute-start | bytes 786440 | tf_op jit(solution)/shard_map/ppermute | solution.py:292
  50.6 13.0 %copy-start.18 = (bf16[256,512]{1,0:T(8,128)(2,1)}, bf16[256,512]{1,0:T(8,128)(2,1)S(1)}, u32[]{:S(2)}) copy-start(bf16[256,512]{1,0:T(8,128)(2,1)S(1)} %collective-permute-done.8.refs_7_) | copy-start | bytes 786436
  50.6 13.1 %collective-permute-start.5 = (bf16[256,512]{1,0:T(8,128)(2,1)S(1)}, bf16[256,512]{1,0:T(8,128)(2,1)}, u32[]{:S(2)}, u32[]{:S(2)}) collective-permute-start(bf16[256,512]{1,0:T(8,128)(2,1)S(1)} %collective-permute-done.3.refs_2_), channel_id=1, source_target_pairs={{0,2},{2,0},{4,6},{6,4},{8,10},{10,8},{12,14},{14,12},{16,18},{18,... | collective-permute-start | bytes 786440 | tf_op jit(solution)/shard_map/ppermute | solution.py:292
  50.7 13.0 %collective-permute-start.12 = (bf16[256,512]{1,0:T(8,128)(2,1)S(1)}, bf16[256,512]{1,0:T(8,128)(2,1)}, u32[]{:S(2)}, u32[]{:S(2)}) collective-permute-start(bf16[256,512]{1,0:T(8,128)(2,1)S(1)} %collective-permute-done.10.refs_9_), channel_id=1, source_target_pairs={{0,2},{2,0},{4,6},{6,4},{8,10},{10,8},{12,14},{14,12},{16,18},{18,... | collective-permute-start | bytes 786440 | tf_op jit(solution)/shard_map/ppermute | solution.py:292
  63.6 0.8 copy-start.19
  63.6 0.9 copy-start.20
  63.6 0.7 copy-start.21
  64.5 33.1 %copy-start.5 = (bf16[1,1024,512]{2,1,0:T(8,128)(2,1)S(1)}, bf16[1,1024,512]{2,1,0:T(8,128)(2,1)}, u32[]{:S(2)}) copy-start(bf16[1,1024,512]{2,1,0:T(8,128)(2,1)} %get-tuple-element.30.n_own_ref) | copy-start | bytes 3145732
  64.5 40.3 %copy-start.7 = (s32[2]{0:T(128)S(1)}, s32[2]{0:T(128)}, u32[]{:S(2)}) copy-start(s32[2]{0:T(128)} %pad_add_fusion.1.half_ref.refs_0_.scal_ref) | copy-start | bytes 28
  97.4 17.3 %collective-permute-start.21 = (bf16[3,1024,512]{2,1,0:T(8,128)(2,1)}, bf16[3,1024,512]{2,1,0:T(8,128)(2,1)S(1)}, u32[]{:S(2)}, u32[]{:S(2)}) collective-permute-start(bf16[3,1024,512]{2,1,0:T(8,128)(2,1)} %get-tuple-element.29.n_own_ref), channel_id=1, source_target_pairs={{0,2},{2,0},{4,6},{6,4},{8,10},{10,8},{12,14},{14,12},{16,18},{18,... | collective-permute-start | bytes 9437192 | tf_op jit(solution)/shard_map/ppermute | solution.py:292
  97.6 17.1 %copy-start.6 = (s32[4]{0:T(128)S(1)}, s32[4]{0:T(128)}, u32[]{:S(2)}) copy-start(s32[4]{0:T(128)} %pad_add_fusion.refs_0_.scal_ref) | copy-start | bytes 52
  97.6 7.2 %collective-permute-start.22 = (bf16[1,1024,512]{2,1,0:T(8,128)(2,1)S(1)}, bf16[1,1024,512]{2,1,0:T(8,128)(2,1)S(1)}, u32[]{:S(2)}, u32[]{:S(2)}) collective-permute-start(bf16[1,1024,512]{2,1,0:T(8,128)(2,1)S(1)} %copy-done.5), channel_id=1, source_target_pairs={{0,2},{2,0},{4,6},{6,4},{8,10},{10,8},{12,14},{14,12},{16,18},{18,... | collective-permute-start | bytes 3145736 | tf_op jit(solution)/shard_map/ppermute | solution.py:292
  104.8 2.2 %copy-start = (bf16[4,512,1024]{2,1,0:T(8,128)(2,1)S(1)}, bf16[4,512,1024]{2,1,0:T(8,128)(2,1)}, u32[]{:S(2)}) copy-start(bf16[4,512,1024]{2,1,0:T(8,128)(2,1)} %q_other_ref.3) | copy-start | bytes 12582916
  107.0 2.2 %copy-start.2 = (bf16[4,512,1024]{2,1,0:T(8,128)(2,1)S(1)}, bf16[4,512,1024]{2,1,0:T(8,128)(2,1)}, u32[]{:S(2)}) copy-start(bf16[4,512,1024]{2,1,0:T(8,128)(2,1)} %ql_own_ref.3) | copy-start | bytes 12582916
  109.2 5.5 %copy-start.1 = (bf16[4,512,1024]{2,1,0:T(8,128)(2,1)S(1)}, bf16[4,512,1024]{2,1,0:T(8,128)(2,1)}, u32[]{:S(2)}) copy-start(bf16[4,512,1024]{2,1,0:T(8,128)(2,1)} %q_other_ref.3) | copy-start | bytes 12582916
  109.2 5.5 %copy-start.3 = (bf16[4,512,1024]{2,1,0:T(8,128)(2,1)S(1)}, bf16[4,512,1024]{2,1,0:T(8,128)(2,1)}, u32[]{:S(2)}) copy-start(bf16[4,512,1024]{2,1,0:T(8,128)(2,1)} %ql_own_ref.3) | copy-start | bytes 12582916
  109.2 5.5 %copy-start.4 = (bf16[3,1024,512]{2,1,0:T(8,128)(2,1)S(1)}, bf16[3,1024,512]{2,1,0:T(8,128)(2,1)}, u32[]{:S(2)}) copy-start(bf16[3,1024,512]{2,1,0:T(8,128)(2,1)} %get-tuple-element.29.n_own_ref) | copy-start | bytes 9437188
